TPU v7x, 128 devices: a whole 4x4x4 slice. The times are simulated.
128 devices in a mesh: req: 16 (over z, x), tok: 8 (over y, core).
Axes of the slice: x: 4, y: 4, z: 4, core: 2. Of those that a mesh axis runs over, the one named last changes fastest.
Arguments:
- queries: bfloat16 [8192, 2048], P('req', 'tok'), may hold values from -6 to 6
- suffix_kv: bfloat16 [8192, 2048], P('req'), may hold values from -6 to 6
- prefix_cache: bfloat16 [8192, 2048], P('req'), may hold values from -24 to 24
- q_gain: float32 [256], replicated, may hold values from 0.1 to 1.9
- k_gain: float32 [256], replicated, may hold values from 0.1 to 1.9
- lengths: int32 [16, 3], P('req'), may hold values from 1 to 256, 512 in all within a row
- group_of: int32 [16], replicated, may hold values from 0 to 1
- owner_order: int32 [16], replicated, may hold values from 0 to 15, each once
- residual: bfloat16 [8192, 2560], P('req'), may hold values from -6 to 6
- w_out: bfloat16 [2048, 2560], P('tok'), may hold values from -0.125 to 0.125
- attn_gain: float32 [2560], replicated, may hold values from 0.1 to 1.9
- ffn_in_gain: float32 [2560], replicated, may hold values from 0.1 to 1.9
- ffn_out_gain: float32 [2560], replicated, may hold values from 0.1 to 1.9
- w_gate: bfloat16 [2560, 10240], P(None, 'tok'), may hold values from -0.125 to 0.125
- w_up: bfloat16 [2560, 10240], P(None, 'tok'), may hold values from -0.125 to 0.125
- w_down: bfloat16 [10240, 2560], P('tok'), may hold values from -0.0625 to 0.0625
Outputs:
- layer_out: bfloat16 [8192, 2560], P(('req', 'tok'))
Inputs may be any that keep to these rules, and one draw needn't show every extreme that they name: The 3 lengths of each req index sum to 512; the largest is exactly 256. `owner_order`: each req index appears once; entries g * 8 to g * 8 + 7 name the holders of group g's prefix.
All inputs are finite; a program needn't handle non-finite values.
Results may differ from a plain program's by a relative error of at most 0.02.
Values may be sent and summed in bfloat16 or wider, within the bound.
A program may use at most 128 MiB of HBM per device.

v0:
```python
import jax
import jax.numpy as jnp
from jax import lax
from jax.sharding import PartitionSpec as P

H = 8
KVH = 4
HD = 256
GROUPS = 2
EPSILON = 1e-06
MASKED = -1e30


def rms_scale(values_in, gain_vec):
    return (
        values_in
        * lax.rsqrt(jnp.mean(values_in * values_in, axis=-1, keepdims=True) + EPSILON)
        * gain_vec
    )


def norm_heads(values_in, gain_vec, head_count):
    row_count = values_in.shape[0]
    shaped = values_in.astype(jnp.float32).reshape(row_count, head_count, HD)
    return rms_scale(shaped, gain_vec).astype(jnp.bfloat16).reshape(row_count, head_count * HD)


def local(
    queries,
    suffix_kv,
    prefix_cache,
    q_gain,
    k_gain,
    lengths,
    group_of,
    owner_order,
    residual,
    w_out,
    attn_gain,
    ffn_in_gain,
    ffn_out_gain,
    w_gate,
    w_up,
    w_down,
):
    req_count = lax.axis_size("req")
    tok_count = lax.axis_size("tok")
    req_index = lax.axis_index("req")
    tok_index = lax.axis_index("tok")
    row_count = queries.shape[0]
    heads_here = queries.shape[1] // HD
    head_ratio = H // KVH
    kv_first = tok_index * heads_here // head_ratio
    kv_width = KVH * HD
    own_count = req_count // GROUPS
    with jax.named_scope("prefix_gather"):
        pref_keys = lax.dynamic_slice_in_dim(prefix_cache, kv_first * HD, HD, 1)
        pref_vals = lax.dynamic_slice_in_dim(prefix_cache, kv_width + kv_first * HD, HD, 1)
        pref_kv = jnp.concatenate([pref_keys, pref_vals], axis=1)
        gathered = lax.all_gather(pref_kv, "req", axis=0, tiled=False)
        own_group = group_of[req_index]
        owner_ids = lax.dynamic_slice_in_dim(owner_order, own_group * own_count, own_count)
        shared = jnp.take(gathered, owner_ids, axis=0).reshape(-1, 2 * HD)
    with jax.named_scope("attention"):
        query_normed = norm_heads(queries, q_gain, heads_here)
        suf_keys = norm_heads(lax.dynamic_slice_in_dim(suffix_kv, kv_first * HD, HD, 1), k_gain, 1)
        suf_vals = lax.dynamic_slice_in_dim(suffix_kv, kv_width + kv_first * HD, HD, 1)
        all_keys = jnp.concatenate([shared[:, :HD], suf_keys], axis=0)
        all_vals = jnp.concatenate([shared[:, HD:], suf_vals], axis=0)
        seg_ends = jnp.cumsum(lengths[0])
        positions = jnp.arange(row_count, dtype=jnp.int32)
        segment = jnp.sum((positions[:, None] >= seg_ends[None, :]).astype(jnp.int32), axis=1)
        causal = (segment[:, None] == segment[None, :]) & (positions[None, :] <= positions[:, None])
        visible = jnp.concatenate(
            [jnp.ones((row_count, shared.shape[0]), jnp.bool_), causal], axis=1
        )
        outputs = []
        for head_idx in range(heads_here):
            head_q = query_normed[:, head_idx * HD : (head_idx + 1) * HD]
            scores = jnp.dot(head_q, all_keys.T, preferred_element_type=jnp.float32) * HD ** (-0.5)
            scores = jnp.where(visible, scores, MASKED)
            row_max = jnp.max(scores, axis=-1, keepdims=True)
            weights = jnp.exp(scores - row_max)
            row_sum = jnp.sum(weights, axis=-1, keepdims=True)
            head_out = (
                jnp.dot(weights.astype(jnp.bfloat16), all_vals, preferred_element_type=jnp.float32)
                / row_sum
            )
            outputs.append(head_out)
        attention = jnp.concatenate(outputs, axis=1).astype(jnp.bfloat16)
    share = row_count // tok_count
    first_row = tok_index * share
    with jax.named_scope("out_projection"):
        projected = lax.psum_scatter(
            jnp.dot(attention, w_out, preferred_element_type=jnp.float32),
            "tok",
            scatter_dimension=0,
            tiled=True,
        )
        residual_share = lax.dynamic_slice_in_dim(residual, first_row, share, 0)
        mixed_share = residual_share.astype(jnp.float32) + rms_scale(projected, attn_gain)
        normed_share = rms_scale(mixed_share, ffn_in_gain).astype(jnp.bfloat16)
        normed = lax.all_gather(normed_share, "tok", axis=0, tiled=True)
    with jax.named_scope("feed_forward"):
        gate = jnp.dot(normed, w_gate, preferred_element_type=jnp.float32)
        upward = jnp.dot(normed, w_up, preferred_element_type=jnp.float32)
        hidden = (jax.nn.gelu(gate, approximate=True) * upward).astype(jnp.bfloat16)
        down_share = lax.psum_scatter(
            jnp.dot(hidden, w_down, preferred_element_type=jnp.float32),
            "tok",
            scatter_dimension=0,
            tiled=True,
        )
    return (mixed_share + rms_scale(down_share, ffn_out_gain)).astype(jnp.bfloat16)


def solution(mesh):
    in_specs = (
        P("req", "tok"),
        P("req", None),
        P("req", None),
        P(),
        P(),
        P("req", None),
        P(),
        P(),
        P("req", None),
        P("tok", None),
        P(),
        P(),
        P(),
        P(None, "tok"),
        P(None, "tok"),
        P("tok", None),
    )
    out_specs = P(("req", "tok"), None)
    return jax.shard_map(local, mesh=mesh, in_specs=in_specs, out_specs=out_specs, check_vma=False)
```

profile of v0, /device:TPU:0, one launch (start us, length us, event | category | flops | bytes accessed | tf_op | source)
XLA Modules:
  0.0 253.7 jit_solution(10753798629921114018)
XLA Ops:
  6.5 0.0 copy-start
  6.5 0.0 copy-start.14
  6.5 0.0 copy-start.15
  6.5 0.0 copy-start.12
  6.5 0.0 copy-start.5
  6.6 0.0 copy-start.11
  6.6 0.0 all-gather.6.cloned.1.call-start
  6.6 2.0 constant_dynamic-slice_fusion.2
  8.6 0.9 pad_maximum_fusion
  9.5 0.0 all-gather.6.cloned.1.call-update
  9.5 0.0 reduce-scatter.3.cloned.1.call-start
  9.6 0.0 copy-done.14
  9.6 0.6 dynamic_slice.22
  10.8 0.0 copy-done.15
  10.9 0.2 reduce-window.8
  11.0 0.0 copy-done.12
  11.0 0.1 compare_and_fusion
  11.1 0.1 broadcast_bitcast_fusion
  11.2 1.1 fusion.39
  12.3 0.1 convert_reduce_fusion
  12.4 0.0 copy-done.5
  12.4 0.1 fusion.36
  12.6 0.0 copy-done.11
  12.6 1.8 fusion.41
  14.4 0.9 fusion.19
  15.3 67.7 %all-gather.6.cloned.1.call-done = bf16[8192,512]{1,0:T(8,128)(2,1)} async-done(((bf16[512,512]{1,0:T(8,128)(2,1)}), bf16[8192,512]{1,0:T(8,128)(2,1)}) %all-gather.6.cloned.1.call-update) | async-done | bytes 8388624 | tf_op jit(solution)/shard_map/prefix_gather/all_gather | solution.py:60
  83.0 6.2 %gather_fusion = bf16[8,512,512]{2,1,0:T(8,128)(2,1)} fusion(bf16[16,512,512]{2,1,0:T(8,128)(2,1)} %bitcast.15, s32[1024]{0:T(1024)S(1)} %pad_clamp_fusion), kind=kCustom, calls=%fused_computation | custom fusion | bytes 8388640 | tf_op jit(solution)/shard_map/prefix_gather/jit(_take)/gather | solution.py:63
  89.2 2.6 %bitcast_select_fusion = bf16[4096,512]{1,0:T(8,128)(2,1)S(1)} fusion(bf16[8,512,512]{2,1,0:T(8,128)(2,1)} %gather_fusion, pred[4096]{0:T(1024)(128)(4,1)S(1)} %bitcast.16), kind=kLoop, calls=%fused_computation.7 | loop fusion | flops 2097152 | bytes 8392704 | tf_op jit(solution)/shard_map/prefix_gather/jit(_take)/select_n | solution.py:63
  91.8 0.0 copy-start.4
  91.8 0.0 copy-start.6
  91.8 0.0 copy-start.7
  91.8 0.0 copy-start.13
  91.8 0.3 fusion.53
  92.1 0.6 copy-done.4
  92.7 0.1 copy-done.6
  92.8 0.1 copy-done.7
  92.9 0.0 copy-done.13
  92.9 1.6 fusion.54
  94.4 0.0 copy-start.2
  94.5 1.4 fusion
  95.9 2.2 copy-done.2
  98.1 0.0 copy-done
  98.1 9.5 %fusion.32 = f32[512,2560]{1,0:T(8,128)} fusion(bf16[256,2560]{1,0:T(8,128)(2,1)S(1)} %copy-done, bf16[512,256]{1,0:T(8,128)(2,1)} %get-tuple-element.13, bf16[4096,256]{1,0:T(8,128)(2,1)S(1)} %get-tuple-element.8, f32[512,4608]{1,0:T(8,128)} %copy-done.2, f32[512]{0:T(512)S(1)} %get-tuple-element.11, f32[512]{0:T(512)S(1)} %fusion), kind=kOutput, calls=%fused_computation.28 | convolution fusion | flops 1888747520 | bytes 18354176 | tf_op jit(solution)/shard_map/out_projection/dot_general | solution.py:95
  107.6 0.0 reduce-scatter.3.cloned.1.call-update
  107.7 0.0 all-gather.4.cloned.1.call-start
  107.7 39.6 %reduce-scatter.3.cloned.1.call-done = f32[64,2560]{1,0:T(8,128)} async-done(((f32[512,2560]{1,0:T(8,128)}), f32[64,2560]{1,0:T(8,128)}) %reduce-scatter.3.cloned.1.call-update) | async-done | bytes 655376 | tf_op jit(solution)/shard_map/out_projection/reduce_scatter | solution.py:94
  147.3 1.2 multiply_reduce_fusion.2
  148.5 0.0 copy-done.8
  148.5 1.5 multiply_reduce_fusion.1
  150.0 0.0 copy-done.9
  150.0 2.1 multiply_convert_fusion
  152.2 0.0 all-gather.4.cloned.1.call-update
  152.2 0.2 reduce-scatter.5.cloned.1.call-start
  152.4 25.6 %all-gather.4.cloned.1.call-done = bf16[512,2560]{1,0:T(8,128)(2,1)} async-done(((bf16[64,2560]{1,0:T(8,128)(2,1)}), bf16[512,2560]{1,0:T(8,128)(2,1)}) %all-gather.4.cloned.1.call-update) | async-done | bytes 2621456 | tf_op jit(solution)/shard_map/out_projection/all_gather | solution.py:103
  178.0 8.8 %fusion.55 = f32[512,1280]{1,0:T(8,128)} fusion(bf16[512,2560]{1,0:T(8,128)(2,1)} %all-gather.4.cloned.1.call-done, bf16[2560,1280]{1,0:T(8,128)(2,1)} %param.29), kind=kOutput, calls=%fused_computation.72 | convolution fusion | flops 3355443200 | bytes 11796480 | tf_op jit(solution)/shard_map/feed_forward/dot_general | solution.py:105
  186.7 16.5 %fusion.35 = f32[512,2560]{1,0:T(8,128)} fusion(bf16[1280,2560]{1,0:T(8,128)(2,1)} %param.31, bf16[512,2560]{1,0:T(8,128)(2,1)} %all-gather.4.cloned.1.call-done, bf16[2560,1280]{1,0:T(8,128)(2,1)} %param.30, f32[512,1280]{1,0:T(8,128)} %fusion.55), kind=kOutput, calls=%fused_computation.29 | convolution fusion | flops 6717440000 | bytes 23592960 | tf_op jit(solution)/shard_map/feed_forward/dot_general | solution.py:109
  203.2 0.0 reduce-scatter.5.cloned.1.call-update
  203.2 0.0 copy-start.1
  203.2 40.6 %reduce-scatter.5.cloned.1.call-done = f32[64,2560]{1,0:T(8,128)} async-done(((f32[512,2560]{1,0:T(8,128)}), f32[64,2560]{1,0:T(8,128)}) %reduce-scatter.5.cloned.1.call-update) | async-done | bytes 655376 | tf_op jit(solution)/shard_map/feed_forward/reduce_scatter | solution.py:108
  243.8 1.2 multiply_reduce_fusion
  245.0 0.0 copy-done.3
  245.0 0.0 copy-done.10
  245.0 2.2 add_convert_fusion
  247.2 0.0 copy-done.1
  (11 shorter events, 0.1 us)
Async XLA Ops:
  6.5 91.5 %copy-start = (bf16[256,2560]{1,0:T(8,128)(2,1)S(1)}, bf16[256,2560]{1,0:T(8,128)(2,1)}, u32[]{:S(2)}) copy-start(bf16[256,2560]{1,0:T(8,128)(2,1)} %param.25) | copy-start | bytes 3932164
  6.5 3.0 %copy-start.14 = (s32[16]{0:T(128)S(1)}, s32[16]{0:T(128)}, u32[]{:S(2)}) copy-start(s32[16]{0:T(128)} %param.22) | copy-start | bytes 196
  6.5 4.3 %copy-start.15 = (s32[1,3]{1,0:T(1,128)S(1)}, s32[1,3]{1,0:T(1,128)}, u32[]{:S(2)}) copy-start(s32[1,3]{1,0:T(1,128)} %param.21) | copy-start | bytes 40
  6.5 4.5 %copy-start.12 = (s32[16]{0:T(128)S(1)}, s32[16]{0:T(128)}, u32[]{:S(2)}) copy-start(s32[16]{0:T(128)} %param.23) | copy-start | bytes 196
  6.5 5.9 %copy-start.5 = (bf16[512,256]{1,0:T(8,128)(2,1)S(1)}, bf16[512,256]{1,0:T(8,128)(2,1)}, u32[]{:S(2)}) copy-start(bf16[512,256]{1,0:T(8,128)(2,1)} %param.16) | copy-start | bytes 786436
  6.6 6.0 %copy-start.11 = (f32[256]{0:T(256)S(1)}, f32[256]{0:T(256)}, u32[]{:S(2)}) copy-start(f32[256]{0:T(256)} %param.20) | copy-start | bytes 3076
  6.6 76.4 %all-gather.6.cloned.1.call-start = ((), (), s32[]{:S(2)}) async-start(), calls=%async_computation.5 | async-start | bytes 8912896 | tf_op jit(solution)/shard_map/prefix_gather/all_gather | solution.py:60
  9.5 137.8 %reduce-scatter.3.cloned.1.call-start = ((), (), s32[]{:S(2)}) async-start(), calls=%async_computation.2 | async-start | bytes 5898240 | tf_op jit(solution)/shard_map/out_projection/reduce_scatter | solution.py:94
  91.8 1.0 copy-start.4
  91.8 1.0 copy-start.6
  91.8 1.1 copy-start.7
  91.8 1.1 copy-start.13
  94.4 3.6 %copy-start.2 = (f32[512,4608]{1,0:T(8,128)}, f32[512,4608]{1,0:T(8,128)S(1)}, u32[]{:S(2)}) copy-start(f32[512,4608]{1,0:T(8,128)S(1)} %get-tuple-element.12) | copy-start | bytes 28311556
  107.6 40.9 %copy-start.8 = (f32[2560]{0:T(1024)S(1)}, f32[2560]{0:T(1024)}, u32[]{:S(2)}) copy-start(f32[2560]{0:T(1024)} %param.26) | copy-start | bytes 30724
  107.6 42.4 %copy-start.9 = (f32[2560]{0:T(1024)S(1)}, f32[2560]{0:T(1024)}, u32[]{:S(2)}) copy-start(f32[2560]{0:T(1024)} %param.27) | copy-start | bytes 30724
  107.7 70.3 %all-gather.4.cloned.1.call-start = ((), (), s32[]{:S(2)}) async-start(), calls=%async_computation.3 | async-start | bytes 2949120 | tf_op jit(solution)/shard_map/out_projection/all_gather | solution.py:103
  152.2 91.6 %reduce-scatter.5.cloned.1.call-start = ((), (), s32[]{:S(2)}) async-start(), calls=%async_computation.4 | async-start | bytes 5898240 | tf_op jit(solution)/shard_map/feed_forward/reduce_scatter | solution.py:108
  203.2 41.8 %copy-start.3 = (f32[64,2560]{1,0:T(8,128)S(1)}, f32[64,2560]{1,0:T(8,128)}, u32[]{:S(2)}) copy-start(f32[64,2560]{1,0:T(8,128)} %reduce-scatter.3.cloned.1.call-done) | copy-start | bytes 1966084
  203.2 41.8 %copy-start.10 = (f32[2560]{0:T(1024)S(1)}, f32[2560]{0:T(1024)}, u32[]{:S(2)}) copy-start(f32[2560]{0:T(1024)} %param.28) | copy-start | bytes 30724
  203.2 44.0 %copy-start.1 = (bf16[256,2560]{1,0:T(8,128)(2,1)S(1)}, bf16[256,2560]{1,0:T(8,128)(2,1)}, u32[]{:S(2)}) copy-start(bf16[256,2560]{1,0:T(8,128)(2,1)} %param.25) | copy-start | bytes 3932164
Sparse Core Ops, SparseCore 0:
  9.6 73.3 all-gather.5
  107.8 39.4 reduce-scatter.2
  152.3 25.6 all-gather.3
  203.3 40.3 reduce-scatter.4
where the time goes:
time: 254 us
  waiting for transfers between devices  173 us (68%)
  matrix products  36.3 us (14%)
  other arithmetic  17.4 us (7%)
  between operations  14 us (6%)
  local copies, waits for them, and re-layouts  12.2 us (5%)
    all_gather x1, waiting for transfers between devices, local(): gathered = lax.all_gather(pref_kv, 'req', axis=0, tiled=False)  67.7 us
    reduce_scatter x1, waiting for transfers between devices, local(): lax.psum_scatter(jnp.dot(hidden, w_down, preferred_element_type=jnp.float...  40.6 us
    reduce_scatter x1, waiting for transfers between devices, local(): lax.psum_scatter(jnp.dot(attention, w_out, preferred_element_type=jnp.flo...  39.6 us
    all_gather x1, waiting for transfers between devices, local(): normed = lax.all_gather(normed_share, 'tok', axis=0, tiled=True)  25.6 us
    dot_general x1, matrix products, local(): jnp.dot(hidden, w_down, preferred_element_type=jnp.float32)  16.5 us
    dot_general x1, matrix products, local(): jnp.dot(attention, w_out, preferred_element_type=jnp.float32)  9.55 us
    dot_general x1, matrix products, local(): gate = jnp.dot(normed, w_gate, preferred_element_type=jnp.float32)  8.76 us
    gather x1, local copies, waits for them, and re-layouts, local(): shared = jnp.take(gathered, owner_ids, axis=0).reshape(-1, 2 * HD)  6.17 us
  transfers between devices with their start and end apart: 4, of which 4 were waited for; matrix products, arithmetic and copies ran while one was open for 2% of the time, Pallas kernels for 0%

commit v1 on v0

--- a/solution.py
+++ b/solution.py
@@ -100,7 +100,8 @@
         residual_share = lax.dynamic_slice_in_dim(residual, first_row, share, 0)
         mixed_share = residual_share.astype(jnp.float32) + rms_scale(projected, attn_gain)
         normed_share = rms_scale(mixed_share, ffn_in_gain).astype(jnp.bfloat16)
-        normed = lax.all_gather(normed_share, "tok", axis=0, tiled=True)
+        repeated = jnp.stack([normed_share] * lax.axis_size("tok"))
+        normed = jnp.concatenate(lax.all_to_all(repeated, "tok", 0, 0), axis=0)
     with jax.named_scope("feed_forward"):
         gate = jnp.dot(normed, w_gate, preferred_element_type=jnp.float32)
         upward = jnp.dot(normed, w_up, preferred_element_type=jnp.float32)

time: 254 us -> 263 us (1.035)
  blocking collectives: 0 us -> 35.7 us
  waiting for transfers between devices: 173 us -> 147 us
    all_to_all x0 -> x1, blocking collectives: none -> 35.7 us  [local(): normed = jnp.concatenate(lax.all_to_all(repeated, 'tok', 0, 0), axis=0)]
    all_gather x1 -> x0, waiting for transfers between devices: 25.6 us -> none  [local(): normed = lax.all_gather(normed_share, 'tok', axis=0, tiled=True)]
  transfers between devices with their start and end apart: 4 -> 3, of which waited for: 4 -> 3; matrix products, arithmetic and copies ran while one was open for 2% -> 2% of each run, Pallas kernels for 0% -> 0%
where the time goes in v1:
time: 263 us
  waiting for transfers between devices  147 us (56%)
  blocking collectives  35.7 us (14%)
  matrix products  35.5 us (13%)
  other arithmetic  16.7 us (6%)
  between operations  14 us (5%)
  local copies, waits for them, and re-layouts  13.9 us (5%)
    all_gather x1, waiting for transfers between devices, local(): gathered = lax.all_gather(pref_kv, 'req', axis=0, tiled=False)  67.7 us
    reduce_scatter x1, waiting for transfers between devices, local(): lax.psum_scatter(jnp.dot(attention, w_out, preferred_element_type=jnp.flo...  39.6 us
    reduce_scatter x1, waiting for transfers between devices, local(): lax.psum_scatter(jnp.dot(hidden, w_down, preferred_element_type=jnp.float...  39.4 us
    all_to_all x1, blocking collectives, local(): normed = jnp.concatenate(lax.all_to_all(repeated, 'tok', 0, 0), axis=0)  35.7 us
    dot_general x1, matrix products, local(): jnp.dot(hidden, w_down, preferred_element_type=jnp.float32)  16.5 us
    dot_general x1, matrix products, local(): jnp.dot(attention, w_out, preferred_element_type=jnp.float32)  9.55 us
    dot_general x1, matrix products, local(): gate = jnp.dot(normed, w_gate, preferred_element_type=jnp.float32)  7.96 us
    gather x1, local copies, waits for them, and re-layouts, local(): shared = jnp.take(gathered, owner_ids, axis=0).reshape(-1, 2 * HD)  6.17 us
  transfers between devices with their start and end apart: 3, of which 3 were waited for; matrix products, arithmetic and copies ran while one was open for 2% of the time, Pallas kernels for 0%

profile of v1, /device:TPU:0, one launch (start us, length us, event | category | flops | bytes accessed | tf_op | source)
XLA Modules:
  0.0 262.7 jit_solution(6977417055777922550)
XLA Ops:
  6.5 0.0 copy-start
  6.5 0.0 copy-start.15
  6.5 0.0 copy-start.16
  6.5 0.0 copy-start.13
  6.5 0.0 copy-start.6
  6.6 0.0 copy-start.12
  6.6 0.0 all-gather.3.cloned.1.call-start
  6.6 2.0 constant_dynamic-slice_fusion.2
  8.6 0.9 pad_maximum_fusion
  9.5 0.0 all-gather.3.cloned.1.call-update
  9.5 0.0 reduce-scatter.3.cloned.1.call-start
  9.6 0.0 copy-done.15
  9.6 0.6 dynamic_slice.22
  10.8 0.0 copy-done.16
  10.9 0.2 reduce-window.8
  11.0 0.0 copy-done.13
  11.0 0.1 compare_and_fusion
  11.1 0.1 broadcast_bitcast_fusion
  11.2 1.1 fusion.39
  12.3 0.1 convert_reduce_fusion
  12.4 0.0 copy-done.6
  12.4 0.1 fusion.36
  12.6 0.0 copy-done.12
  12.6 1.8 fusion.41
  14.4 0.9 fusion.19
  15.3 67.7 %all-gather.3.cloned.1.call-done = bf16[8192,512]{1,0:T(8,128)(2,1)} async-done(((bf16[512,512]{1,0:T(8,128)(2,1)}), bf16[8192,512]{1,0:T(8,128)(2,1)}) %all-gather.3.cloned.1.call-update) | async-done | bytes 8388624 | tf_op jit(solution)/shard_map/prefix_gather/all_gather | solution.py:60
  83.0 6.2 %gather_fusion = bf16[8,512,512]{2,1,0:T(8,128)(2,1)} fusion(bf16[16,512,512]{2,1,0:T(8,128)(2,1)} %bitcast.18, s32[1024]{0:T(1024)S(1)} %pad_clamp_fusion), kind=kCustom, calls=%fused_computation | custom fusion | bytes 8388640 | tf_op jit(solution)/shard_map/prefix_gather/jit(_take)/gather | solution.py:63
  89.2 2.6 bitcast_select_fusion
  91.8 0.0 copy-start.5
  91.8 0.0 copy-start.7
  91.8 0.0 copy-start.8
  91.8 0.0 copy-start.14
  91.8 0.3 fusion.53
  92.1 0.6 copy-done.5
  92.7 0.1 copy-done.7
  92.8 0.1 copy-done.8
  92.9 0.0 copy-done.14
  92.9 1.6 fusion.54
  94.4 0.0 copy-start.2
  94.5 1.4 fusion
  95.9 2.2 copy-done.2
  98.1 0.0 copy-done
  98.1 9.5 %fusion.32 = f32[512,2560]{1,0:T(8,128)} fusion(bf16[256,2560]{1,0:T(8,128)(2,1)S(1)} %copy-done, bf16[512,256]{1,0:T(8,128)(2,1)} %get-tuple-element.13, bf16[4096,256]{1,0:T(8,128)(2,1)S(1)} %get-tuple-element.8, f32[512,4608]{1,0:T(8,128)} %copy-done.2, f32[512]{0:T(512)S(1)} %get-tuple-element.11, f32[512]{0:T(512)S(1)} %fusion), kind=kOutput, calls=%fused_computation.28 | convolution fusion | flops 1888747520 | bytes 18354176 | tf_op jit(solution)/shard_map/out_projection/dot_general | solution.py:95
  107.6 0.0 reduce-scatter.3.cloned.1.call-update
  107.7 0.0 reduce-scatter.5.cloned.1.call-start
  107.7 39.6 %reduce-scatter.3.cloned.1.call-done = f32[64,2560]{1,0:T(8,128)} async-done(((f32[512,2560]{1,0:T(8,128)}), f32[64,2560]{1,0:T(8,128)}) %reduce-scatter.3.cloned.1.call-update) | async-done | bytes 655376 | tf_op jit(solution)/shard_map/out_projection/reduce_scatter | solution.py:94
  147.3 1.2 multiply_reduce_fusion.2
  148.5 0.0 copy-done.9
  148.5 1.5 multiply_reduce_fusion.1
  150.0 0.0 copy-done.10
  150.0 1.4 multiply_convert_fusion
  151.4 0.2 stack.2
  151.7 35.7 %all_to_all.5 = bf16[8,64,2560]{2,1,0:T(8,128)(2,1)S(1)} all-to-all(bf16[8,64,2560]{2,1,0:T(8,128)(2,1)S(1)} %stack.2), channel_id=1, replica_groups=mesh['req'=16,'tok'=8] {'tok'}, dimensions={0} | all-to-all | bytes 5242880 | tf_op jit(solution)/shard_map/out_projection/all_to_all | solution.py:104
  187.3 1.5 copy-done.4
  188.8 8.0 %fusion.55 = f32[512,1280]{1,0:T(8,128)} fusion(bf16[512,2560]{1,0:T(8,128)(2,1)S(1)} %bitcast.16, bf16[2560,1280]{1,0:T(8,128)(2,1)} %param.29), kind=kOutput, calls=%fused_computation.72 | convolution fusion | flops 3355443200 | bytes 11796480 | tf_op jit(solution)/shard_map/feed_forward/dot_general | solution.py:106
  196.8 16.5 %fusion.35 = f32[512,2560]{1,0:T(8,128)} fusion(bf16[1280,2560]{1,0:T(8,128)(2,1)} %param.31, bf16[512,2560]{1,0:T(8,128)(2,1)} %bitcast.17, bf16[2560,1280]{1,0:T(8,128)(2,1)} %param.30, f32[512,1280]{1,0:T(8,128)} %fusion.55), kind=kOutput, calls=%fused_computation.29 | convolution fusion | flops 6717440000 | bytes 23592960 | tf_op jit(solution)/shard_map/feed_forward/dot_general | solution.py:110
  213.3 0.0 reduce-scatter.5.cloned.1.call-update
  213.3 0.0 copy-start.1
  213.3 39.4 %reduce-scatter.5.cloned.1.call-done = f32[64,2560]{1,0:T(8,128)} async-done(((f32[512,2560]{1,0:T(8,128)}), f32[64,2560]{1,0:T(8,128)}) %reduce-scatter.5.cloned.1.call-update) | async-done | bytes 655376 | tf_op jit(solution)/shard_map/feed_forward/reduce_scatter | solution.py:109
  252.7 1.2 multiply_reduce_fusion
  254.0 0.0 copy-done.3
  254.0 0.0 copy-done.11
  254.0 2.2 add_convert_fusion
  256.1 0.0 copy-done.1
  (12 shorter events, 0.1 us)
Async XLA Ops:
  6.5 91.5 %copy-start = (bf16[256,2560]{1,0:T(8,128)(2,1)S(1)}, bf16[256,2560]{1,0:T(8,128)(2,1)}, u32[]{:S(2)}) copy-start(bf16[256,2560]{1,0:T(8,128)(2,1)} %param.25) | copy-start | bytes 3932164
  6.5 3.0 %copy-start.15 = (s32[16]{0:T(128)S(1)}, s32[16]{0:T(128)}, u32[]{:S(2)}) copy-start(s32[16]{0:T(128)} %param.22) | copy-start | bytes 196
  6.5 4.3 %copy-start.16 = (s32[1,3]{1,0:T(1,128)S(1)}, s32[1,3]{1,0:T(1,128)}, u32[]{:S(2)}) copy-start(s32[1,3]{1,0:T(1,128)} %param.21) | copy-start | bytes 40
  6.5 4.5 %copy-start.13 = (s32[16]{0:T(128)S(1)}, s32[16]{0:T(128)}, u32[]{:S(2)}) copy-start(s32[16]{0:T(128)} %param.23) | copy-start | bytes 196
  6.5 5.9 %copy-start.6 = (bf16[512,256]{1,0:T(8,128)(2,1)S(1)}, bf16[512,256]{1,0:T(8,128)(2,1)}, u32[]{:S(2)}) copy-start(bf16[512,256]{1,0:T(8,128)(2,1)} %param.16) | copy-start | bytes 786436
  6.6 6.0 %copy-start.12 = (f32[256]{0:T(256)S(1)}, f32[256]{0:T(256)}, u32[]{:S(2)}) copy-start(f32[256]{0:T(256)} %param.20) | copy-start | bytes 3076
  6.6 76.4 %all-gather.3.cloned.1.call-start = ((), (), s32[]{:S(2)}) async-start(), calls=%async_computation.5 | async-start | bytes 8912896 | tf_op jit(solution)/shard_map/prefix_gather/all_gather | solution.py:60
  9.5 137.8 %reduce-scatter.3.cloned.1.call-start = ((), (), s32[]{:S(2)}) async-start(), calls=%async_computation.3 | async-start | bytes 5898240 | tf_op jit(solution)/shard_map/out_projection/reduce_scatter | solution.py:94
  91.8 1.0 copy-start.5
  91.8 1.0 copy-start.7
  91.8 1.1 copy-start.8
  91.8 1.1 copy-start.14
  94.4 3.6 %copy-start.2 = (f32[512,4608]{1,0:T(8,128)}, f32[512,4608]{1,0:T(8,128)S(1)}, u32[]{:S(2)}) copy-start(f32[512,4608]{1,0:T(8,128)S(1)} %get-tuple-element.12) | copy-start | bytes 28311556
  107.6 40.9 %copy-start.9 = (f32[2560]{0:T(1024)S(1)}, f32[2560]{0:T(1024)}, u32[]{:S(2)}) copy-start(f32[2560]{0:T(1024)} %param.26) | copy-start | bytes 30724
  107.6 42.4 %copy-start.10 = (f32[2560]{0:T(1024)S(1)}, f32[2560]{0:T(1024)}, u32[]{:S(2)}) copy-start(f32[2560]{0:T(1024)} %param.27) | copy-start | bytes 30724
  107.7 145.1 %reduce-scatter.5.cloned.1.call-start = ((), (), s32[]{:S(2)}) async-start(), calls=%async_computation.4 | async-start | bytes 5898240 | tf_op jit(solution)/shard_map/feed_forward/reduce_scatter | solution.py:109
  187.3 1.5 copy-start.4
  213.2 40.7 %copy-start.3 = (f32[64,2560]{1,0:T(8,128)S(1)}, f32[64,2560]{1,0:T(8,128)}, u32[]{:S(2)}) copy-start(f32[64,2560]{1,0:T(8,128)} %reduce-scatter.3.cloned.1.call-done) | copy-start | bytes 1966084
  213.2 40.7 %copy-start.11 = (f32[2560]{0:T(1024)S(1)}, f32[2560]{0:T(1024)}, u32[]{:S(2)}) copy-start(f32[2560]{0:T(1024)} %param.28) | copy-start | bytes 30724
  213.3 42.9 %copy-start.1 = (bf16[256,2560]{1,0:T(8,128)(2,1)S(1)}, bf16[256,2560]{1,0:T(8,128)(2,1)}, u32[]{:S(2)}) copy-start(bf16[256,2560]{1,0:T(8,128)(2,1)} %param.25) | copy-start | bytes 3932164
Sparse Core Ops, SparseCore 0:
  9.6 73.3 all-gather.2
  107.8 39.4 reduce-scatter.2
  213.4 39.2 reduce-scatter.4
